TPU v7x, 32 devices: a whole 2x2x4 slice. The times are simulated.
32 devices in a mesh: groups: 2 (over y), chan: 4 (over z), seg: 2 (over x), freq: 2 (over core).
Axes of the slice: x: 2, y: 2, z: 4, core: 2. Of those that a mesh axis runs over, the one named last changes fastest.
Arguments:
- traces: bfloat16 [10, 1024, 4096], P('seg', ('groups', 'chan')), parts along dimension 1, may hold values from -120 to 120
- dead_mask: int32 [1024], P(('groups', 'chan')), parts along dimension 0, may hold values 0 or 1
- seg_counts: int32 [1024], P(('groups', 'chan')), parts along dimension 0, may hold values from 1 to 10
- offsets: int32 [4], replicated, may hold values from 1 to 128, as said below
Outputs:
- correlations: float32 [1024, 4, 512], P(('groups', 'chan', 'seg'), None, 'freq'), parts along dimension 0
There are 2 independent parts, one for each index of `groups`. A program takes and returns all parts, laid end to end along the dimension named above; an argument that names none is the same for every part. Nothing has to cross between parts.
Inputs may be any that keep to these rules, and one draw needn't show every extreme that they name: The 4 offsets are distinct and one of them equals 128.
All inputs are finite; a program needn't handle non-finite values. No bound on the sum of `dead_mask` on one device may be relied on, other than what follows from the above.
Results may differ from a plain program's by a relative error of at most 0.0056.
Values may be sent and summed in bfloat16 or wider, within the bound.
A program may use at most 128 MiB of HBM per device.

v0:
```python
import math

import jax
import jax.numpy as jnp
from jax import lax
from jax.sharding import PartitionSpec as P

HALF = 32
LAGS = 512
F = 2048


epsilon = 1e-06


def padded(array, sides, width):
    for axis, dim in sides:
        peers, length = (lax.axis_size(axis), array.shape[dim])
        up = [(i, (i + 1) % peers) for i in range(peers - 1)]
        down = [(j, i) for i, j in up]
        last = lax.slice_in_dim(array, length - width, length, axis=dim)
        leading = lax.slice_in_dim(array, 0, width, axis=dim)
        before = lax.ppermute(last, axis, up)
        after = lax.ppermute(leading, axis, down)
        array = jnp.concatenate([before, array, after], axis=dim)
    return array


def from_behind(block, axis, distance):
    devices = range(lax.axis_size(axis))
    route = [(i - distance, i) for i in devices if i - distance in devices]
    return lax.ppermute(block, axis, route)


def fourier_table(bin_first, bin_number, length):
    samples = jnp.arange(length, dtype=jnp.int32)[:, None]
    bin_index = bin_first + jnp.arange(bin_number, dtype=jnp.int32)[None, :]
    phases = (samples * bin_index % length).astype(jnp.float32) * (2.0 * math.pi / length)
    return jnp.concatenate([jnp.cos(phases), -jnp.sin(phases)], axis=1).astype(jnp.bfloat16)


def delay_table(bin_first, bin_number, length, lag_number, bin_total):
    bin_index = bin_first + jnp.arange(bin_number, dtype=jnp.int32)[:, None]
    shifts = jnp.arange(lag_number, dtype=jnp.int32)[None, :] - lag_number // 2
    phases = (bin_index * shifts % length).astype(jnp.float32) * (2.0 * math.pi / length)
    scaling = 1.0 / math.sqrt(bin_total)
    return jnp.concatenate([jnp.cos(phases) * scaling, -jnp.sin(phases) * scaling], axis=0)


def shards(traces, dead_mask, seg_counts, offsets):
    seg_dev, chan_dev, length = traces.shape
    bins_dev = F // lax.axis_size("freq")
    bin_first = lax.axis_index("freq") * bins_dev
    seg_first = lax.axis_index("seg") * seg_dev
    fourier = fourier_table(bin_first, bins_dev, length)
    bin_index = bin_first + jnp.arange(bins_dev, dtype=jnp.int32)
    window_count = (
        jnp.minimum(bin_index + HALF, F - 1) - jnp.maximum(bin_index - HALF, 0) + 1
    ).astype(jnp.float32)
    seg_index = seg_first + jnp.arange(seg_dev, dtype=jnp.int32)
    alive_own = dead_mask.astype(jnp.float32)
    spectra = jnp.dot(
        traces.reshape(seg_dev * chan_dev, length), fourier, preferred_element_type=jnp.float32
    )
    spectra = spectra.reshape(seg_dev, chan_dev, 2 * bins_dev)
    real_part = spectra[:, :, :bins_dev]
    imag_part = spectra[:, :, bins_dev:]
    power_bins = real_part * real_part + imag_part * imag_part
    rimmed = padded(power_bins, (("freq", 2),), HALF)
    window_sum = lax.reduce_window(
        rimmed, jnp.zeros((), rimmed.dtype), lax.add, (1, 1, 2 * HALF + 1), (1, 1, 1), "VALID"
    )
    valid_seg = (seg_index[:, None] < seg_counts[None, :]).astype(jnp.float32) * alive_own[None, :]
    factor = valid_seg[:, :, None] / jnp.sqrt(window_sum / window_count + epsilon)
    white = jnp.concatenate([real_part * factor, imag_part * factor], axis=2)
    own_counts = seg_counts.astype(jnp.float32)
    next_white, next_count_f = from_behind((white, own_counts), "chan", -1)
    combined = jnp.concatenate([white, next_white], axis=1)
    all_counts = jnp.concatenate([own_counts, next_count_f])
    white_re = white[:, :, :bins_dev]
    white_im = white[:, :, bins_dev:]
    slots = []
    for slot in range(offsets.shape[0]):
        offset = offsets[slot]
        partner = lax.dynamic_slice_in_dim(combined, offset, chan_dev, 1)
        partner_re = partner[:, :, :bins_dev]
        partner_im = partner[:, :, bins_dev:]
        cross_spec = jnp.concatenate(
            [
                jnp.sum(white_re * partner_re + white_im * partner_im, axis=0),
                jnp.sum(white_im * partner_re - white_re * partner_im, axis=0),
            ],
            axis=1,
        )
        partner_count = lax.dynamic_slice_in_dim(all_counts, offset, chan_dev, 0)
        divisor = jnp.maximum(jnp.minimum(own_counts, partner_count), 1.0)
        slots.append(cross_spec / divisor[:, None])
    stacked = jnp.stack(slots, axis=1)
    delay = delay_table(bin_first, bins_dev, length, LAGS, F)
    shares = lax.psum_scatter(stacked, "seg", scatter_dimension=0, tiled=True)
    lag_terms = jnp.einsum("ckf,fl->ckl", shares, delay, precision=lax.Precision.HIGHEST)
    return lax.psum_scatter(lag_terms, "freq", scatter_dimension=2, tiled=True)


def solution(mesh):
    in_specs = (
        P("seg", ("groups", "chan"), None),
        P(("groups", "chan")),
        P(("groups", "chan")),
        P(),
    )
    out_specs = P(("groups", "chan", "seg"), None, "freq")
    return jax.shard_map(shards, mesh=mesh, in_specs=in_specs, out_specs=out_specs, check_vma=False)
```

profile of v0, /device:TPU:0, one launch (start us, length us, event | category | flops | bytes accessed | tf_op | source)
XLA Modules:
  0.0 455.6 jit_solution(8970719155979047860)
XLA Ops:
  6.5 0.0 all-reduce.3.cloned.1.call-start
  6.5 69.1 %cosine_convert_fusion = (bf16[4096,1024]{1,0:T(8,128)(2,1)}, bf16[4096,1024]{1,0:T(8,128)(2,1)}) fusion(s32[1024]{0:T(1024)S(1)} %iota_add_fusion), kind=kLoop, calls=%fused_computation.11 | loop fusion | flops 71303168 | bytes 16781312 | tf_op jit(solution)/shard_map/convert
  75.6 17.7 %fusion.3 = f32[2048,640]{0,1:T(8,128)} fusion(bf16[640,4096]{1,0:T(8,128)(2,1)} %bitcast.30, bf16[4096,1024]{1,0:T(8,128)(2,1)} %get-tuple-element.22, bf16[4096,1024]{1,0:T(8,128)(2,1)} %get-tuple-element.21), kind=kOutput, calls=%fused_computation.6 | convolution fusion | flops 10770972672 | bytes 27262976 | tf_op jit(solution)/shard_map/dot_general | solution.py:62
  93.3 5.7 %fusion.21 = (f32[5,128,1024]{2,1,0:T(8,128)}, f32[5,128,1024]{2,1,0:T(8,128)}) fusion(f32[5,128,2048]{2,1,0:T(8,128)} %bitcast.21), kind=kLoop, calls=%fused_computation.63 | loop fusion | bytes 10485760 | tf_op jit(solution)/shard_map/slice | solution.py:66
  99.0 2.1 copy.17
  101.1 0.0 copy-start.1
  101.2 4.2 copy.18
  105.4 2.0 multiply_add_fusion
  107.4 1.5 copy-done.2
  108.9 2.4 collective-permute-start
  111.3 1.5 collective-permute-start.1
  112.8 0.1 compare_select_fusion
  112.9 0.0 collective-permute-done
  112.9 1.6 collective-permute-done.1
  114.5 1.9 pad_maximum_fusion.3
  116.4 45.5 %reduce_window.7 = f32[5,128,1024]{1,2,0:T(8,128)} reduce-window(f32[5,128,1088]{1,2,0:T(8,128)S(1)} %pad_maximum_fusion.3, f32[]{:T(128)} %constant.50.clone.1), window={size=1x1x65}, to_apply=%region_0.1 | reduce-window | flops 41943040 | bytes 5406724 | tf_op jit(solution)/shard_map/reduce_window | solution.py:70
  161.9 4.0 fusion.20
  165.9 0.0 copy-start.7
  165.9 2.9 pad_maximum_fusion.1
  168.8 0.2 copy-done
  169.0 1.3 collective-permute-start.2
  170.3 1.5 collective-permute-start.3
  171.8 0.0 copy-done.7
  171.9 0.7 fusion.23
  180.3 106.7 %collective-permute-done.3 = f32[128]{0:T(128)S(1)} collective-permute-done((f32[128]{0:T(128)S(1)}, f32[128]{0:T(128)S(1)}, u32[]{:S(2)}, u32[]{:S(2)}) %collective-permute-start.3) | collective-permute-done | bytes 544 | tf_op jit(solution)/shard_map/ppermute | solution.py:32
  287.0 0.1 minimum_maximum_fusion.3
  287.1 0.0 collective-permute-done.2
  287.1 8.0 %pad_maximum_fusion = f32[5,256,2048]{1,2,0:T(8,128)} fusion(f32[5,128,2048]{1,2,0:T(8,128)} %collective-permute-done.2, f32[5,128,1024]{1,2,0:T(8,128)} %copy-done, f32[5,128,1024]{1,2,0:T(8,128)S(1)} %get-tuple-element.15), kind=kLoop, calls=%fused_computation.15 | loop fusion | flops 5242880 | bytes 20971520 | tf_op jit(solution)/shard_map/concatenate | solution.py:78
  295.1 17.6 %add_reduce_fusion.3 = (f32[128,1024]{0,1:T(8,128)}, f32[128,1024]{0,1:T(8,128)S(1)}, f32[128,1024]{0,1:T(8,128)}, f32[128,1024]{0,1:T(8,128)}, f32[128,1024]{0,...) fusion(f32[5,128,1024]{1,2,0:T(8,128)} %copy-done, ...), kind=kLoop, calls=%fused_computation.35 | loop fusion | flops 19922944 | bytes 30408724 | tf_op jit(solution)/shard_map/reduce_sum | solution.py:90
  312.7 1.8 maximum_divide_fusion
  314.5 0.0 copy-done.4
  314.5 0.0 copy-done.5
  314.5 0.2 copy-done.6
  314.7 0.2 maximum_divide_fusion.2
  314.8 2.2 pad_maximum_fusion.2
  317.1 5.5 %copy.14 = f32[128,4,2048]{2,1,0:T(4,128)} copy(f32[128,4,2048]{0,2,1:T(8,128)} %pad_maximum_fusion.2) | data formatting | bytes 8388608 | tf_op jit(solution)/shard_map/stack | solution.py:98
  322.6 0.0 all-reduce.3.cloned.1.call-update
  322.6 0.0 reduce-scatter.2.cloned.1.call-start
  322.7 0.6 copy-done.10
  323.2 0.6 dynamic-slice
  324.5 9.7 %cosine_multiply_fusion = (f32[1024,512]{1,0:T(8,128)S(1)}, f32[1024,512]{1,0:T(8,128)}) fusion(s32[512]{0:T(512)S(1)} %iota_add_fusion.1, s32[1024]{0:T(1024)S(1)} %iota_add_fusion), kind=kLoop, calls=%fused_computation.43 | loop fusion | flops 8912896 | bytes 4200448 | tf_op jit(solution)/shard_map/mul | solution.py:47
  334.2 96.8 %all-reduce.3.cloned.1.call-done = f32[128,4,2048]{2,1,0:T(4,128)} async-done(((f32[128,4,2048]{2,1,0:T(4,128)}), f32[128,4,2048]{2,1,0:T(4,128)}) %all-reduce.3.cloned.1.call-update) | async-done | bytes 4194320
  431.0 2.0 constant_dynamic-slice_fusion
  433.0 0.2 copy-done.3
  433.2 5.6 %fusion.10 = f32[64,4,512]{2,0,1:T(8,128)} fusion(f32[1024,512]{1,0:T(8,128)S(1)} %copy-done.3, f32[1024,512]{1,0:T(8,128)S(1)} %get-tuple-element.19, f32[64,4,2048]{2,1,0:T(4,128)S(1)} %constant_dynamic-slice_fusion), kind=kOutput, calls=%fused_computation.19 | convolution fusion | flops 3222274048 | bytes 6815744 | tf_op jit(solution)/shard_map/ckf,fl->ckl/dot_general | solution.py:101
  438.8 0.0 reduce-scatter.2.cloned.1.call-update
  438.8 8.1 %reduce-scatter.2.cloned.1.call-done = f32[64,4,256]{2,0,1:T(8,128)} async-done(((f32[64,4,512]{2,0,1:T(8,128)}), f32[64,4,256]{2,0,1:T(8,128)}) %reduce-scatter.2.cloned.1.call-update) | async-done | bytes 262160 | tf_op jit(solution)/shard_map/reduce_scatter | solution.py:102
  447.0 1.8 copy.16
  (20 shorter events, 0.1 us)
Async XLA Ops:
  6.5 424.5 %all-reduce.3.cloned.1.call-start = ((), (), s32[]{:S(2)}) async-start(), calls=%async_computation.2 | async-start | bytes 8388608
  101.1 4.2 copy-start.1
  105.4 7.4 %copy-start.9 = (s32[128]{0:T(128)S(1)}, s32[128]{0:T(128)}, u32[]{:S(2)}) copy-start(s32[128]{0:T(128)} %param.5) | copy-start | bytes 1540
  105.4 7.5 %copy-start.8 = (s32[128]{0:T(128)S(1)}, s32[128]{0:T(128)}, u32[]{:S(2)}) copy-start(s32[128]{0:T(128)} %param.6) | copy-start | bytes 1540
  107.4 1.5 copy-start.2
  108.9 4.0 collective-permute-start
  111.3 3.2 collective-permute-start.1
  165.9 3.1 copy-start
  165.9 5.9 %copy-start.7 = (s32[4]{0:T(128)S(1)}, s32[4]{0:T(128)}, u32[]{:S(2)}) copy-start(s32[4]{0:T(128)} %param.7) | copy-start | bytes 52
  169.0 118.1 %collective-permute-start.2 = (f32[5,128,2048]{1,2,0:T(8,128)}, f32[5,128,2048]{1,2,0:T(8,128)}, u32[]{:S(2)}, u32[]{:S(2)}) collective-permute-start(f32[5,128,2048]{1,2,0:T(8,128)} %pad_maximum_fusion.1), channel_id=1, source_target_pairs={{4,0},{8,4},{12,8},{5,1},{9,5},{13,9},{6,2},{10,6},{14,10},{7,3},{... | collective-permute-start | bytes 15728648 | tf_op jit(solution)/shard_map/ppermute | solution.py:32
  170.3 116.7 %collective-permute-start.3 = (f32[128]{0:T(128)S(1)}, f32[128]{0:T(128)S(1)}, u32[]{:S(2)}, u32[]{:S(2)}) collective-permute-start(f32[128]{0:T(128)S(1)} %convert_element_type.24), channel_id=1, source_target_pairs={{4,0},{8,4},{12,8},{5,1},{9,5},{13,9},{6,2},{10,6},{14,10},{7,3},{... | collective-permute-start | bytes 1544 | tf_op jit(solution)/shard_map/ppermute | solution.py:32
  312.7 1.8 copy-start.4
  312.7 1.8 copy-start.5
  312.7 2.0 copy-start.6
  322.6 0.7 copy-start.10
  322.6 124.3 %reduce-scatter.2.cloned.1.call-start = ((), (), s32[]{:S(2)}) async-start(), calls=%async_computation.1 | async-start | bytes 786432 | tf_op jit(solution)/shard_map/reduce_scatter | solution.py:102
  431.0 2.2 copy-start.3
Sparse Core Ops, SparseCore 0:
  322.7 108.2 all-reduce.2
  439.0 7.9 reduce-scatter.1
where the time goes:
time: 456 us
  waiting for transfers between devices  213 us (47%)
  other arithmetic  165 us (36%)
  local copies, waits for them, and re-layouts  25.3 us (6%)
  matrix products  23.3 us (5%)
  between operations  22.1 us (5%)
  starting transfers between devices  6.67 us (1%)
    ppermute x2, waiting for transfers between devices, from_behind(): return lax.ppermute(block, axis, route)  107 us
    unnamed x3, waiting for transfers between devices  96.8 us
    another operation x1, other arithmetic  69.1 us
    another operation x1, other arithmetic, shards(): lax.reduce_window(rimmed, jnp.zeros((), rimmed.dtype), lax.add, (1, 1, 2...  45.5 us
    dot_general x1, matrix products, shards(): jnp.dot(traces.reshape(seg_dev * chan_dev, length), fourier, preferred_el...  17.7 us
    reduce_sum x1, other arithmetic, shards(): jnp.sum(white_re * partner_re + white_im * partner_im, axis=0)  17.6 us
    unnamed x26, local copies, waits for them, and re-layouts  11.6 us
    mul x1, other arithmetic, delay_table(): jnp.cos(phases) * scaling  9.73 us
  transfers between devices with their start and end apart: 6, of which 4 were waited for; matrix products, arithmetic and copies ran while one was open for 2% of the time, Pallas kernels for 0%

commit v1 on v0

v1 whole, which is shorter than its diff:
```python
import functools
import math

import jax
import jax.numpy as jnp
import ml_dtypes
import numpy as np
from jax import lax
from jax.experimental import pallas as pl
from jax.experimental.pallas import tpu as pltpu
from jax.sharding import PartitionSpec as P

HALF = 32
LAGS = 512
F = 2048
W = 128
EPS = 1e-06
MESH = pl.DeviceIdType.MESH
F32 = jnp.float32
BF16 = jnp.bfloat16


def bins_of(freq, first, number):
    u = np.arange(first, first + number)
    return u if freq == 0 else F - 1 - u


def fourier_blocks(length, chunks):
    t = np.arange(length // 2)[:, None]
    out = np.empty((2, chunks + 1, length // 2, 2 * W), ml_dtypes.bfloat16)
    cos = np.cos(2.0 * math.pi * np.arange(length) / length)
    sin = np.sin(2.0 * math.pi * np.arange(length) / length)
    for freq in range(2):
        for p in range(chunks + 1):
            phase = t * bins_of(freq, p * W, W)[None, :] % length
            out[freq, p, :, :W] = cos[phase].astype(np.float32).astype(ml_dtypes.bfloat16)
            out[freq, p, :, W:] = (-sin[phase]).astype(np.float32).astype(ml_dtypes.bfloat16)
    return out


def delay_blocks(length, chunks):
    shifts = np.arange(LAGS)[None, :] - LAGS // 2
    out = np.empty((2, chunks, 2 * W, LAGS), ml_dtypes.bfloat16)
    for freq in range(2):
        sign = -1.0 if freq == 0 else 1.0
        for q in range(chunks):
            phase = bins_of(freq, q * W, W)[:, None] * shifts % length * (2.0 * math.pi / length)
            out[freq, q, :W] = (np.cos(phase) / math.sqrt(F)).astype(np.float32)
            out[freq, q, W:] = (sign * np.sin(phase) / math.sqrt(F)).astype(np.float32)
    return out


def dot(a, b):
    return jnp.dot(a, b, preferred_element_type=F32)


def iota(shape, dim):
    return lax.broadcasted_iota(jnp.int32, shape, dim)


def kernel(
    nz, ns, segs, chunks, slots, offs, tr, dead, cnt, four, delay, out,
    table, dly, spec, power, own, recv, sel, mask, total, hoth, hrecv, fsend, frecv, vsum, srecv,
    tab_sem, dly_sem, w_send, w_recv, h_send, h_recv, f_send, f_recv, s_send, s_recv,
):
    z = lax.axis_index("chan")
    s_me = lax.axis_index("seg")
    fq = lax.axis_index("freq")
    up = fq == 1
    half_len = table.shape[1]
    rows = own.shape[1]
    per = W // ns
    step = 2 * fq - 1
    dst = z + step
    src = z - step
    has_dst = jnp.logical_and(dst >= 0, dst < nz)
    has_src = jnp.logical_and(src >= 0, src < nz)
    twin = 1 - fq

    def table_copy(p):
        return pltpu.make_async_copy(four.at[fq, p], table.at[p], tab_sem.at[p])

    for p in range(chunks + 1):
        table_copy(p).start()
    delay_copy = pltpu.make_async_copy(delay.at[fq], dly, dly_sem)
    delay_copy.start()

    barrier = pltpu.get_barrier_semaphore()

    @pl.when(has_dst)
    def _():
        pl.semaphore_signal(barrier, inc=1, device_id={"chan": dst}, device_id_type=MESH)

    @pl.when(has_src)
    def _():
        pl.semaphore_signal(barrier, inc=1, device_id={"chan": src}, device_id_type=MESH)

    pl.semaphore_signal(barrier, inc=1, device_id={"freq": twin}, device_id_type=MESH)
    for d in range(1, ns):
        pl.semaphore_signal(
            barrier, inc=1, device_id={"seg": lax.rem(s_me + d, ns)}, device_id_type=MESH
        )

    peers = ns + has_dst.astype(jnp.int32) + has_src.astype(jnp.int32)
    pl.semaphore_wait(barrier, peers)

    diag = iota((W, W), 0) == iota((W, W), 1)
    cnt_col = jnp.sum(jnp.where(diag, cnt[...], 0).astype(F32), axis=1, keepdims=True)
    live_col = jnp.sum(jnp.where(diag, dead[...], 0).astype(F32), axis=1, keepdims=True)
    for s in range(segs):
        seg_number = (s_me * segs + s).astype(F32)
        valid = jnp.where(seg_number < cnt_col, live_col, 0.0)
        mask[s * W : (s + 1) * W, :] = jnp.broadcast_to(valid, (W, W))
    for k in range(slots):
        target = (iota((W, 2 * W), 0) - step * offs[k] + 2 * W) & (2 * W - 1)
        sel[k * W : (k + 1) * W, :] = jnp.where(iota((W, 2 * W), 1) == target, 1.0, 0.0).astype(BF16)

    @pl.when(jnp.logical_not(has_src))
    def _():
        def clear(q, carry):
            recv[q] = jnp.zeros((rows, 2 * W), BF16)
            return carry

        lax.fori_loop(0, chunks, clear, 0)

    parity = (iota((1, 2 * W), 1) & 1).astype(F32)
    parity = (1.0 - 2.0 * parity) * (1 - 2 * fq).astype(F32)

    def block(p):
        table_copy(p).wait()
        first = dot(tr[:, :half_len], table[p])
        second = dot(tr[:, half_len:], table[p])
        both = first + parity * second
        spec[p] = both
        square = both * both
        power[p + 1] = (square[:, :W] + square[:, W:]).astype(BF16)

    def white_copy(q):
        return pltpu.make_async_remote_copy(
            src_ref=own.at[q], dst_ref=recv.at[q], send_sem=w_send.at[q], recv_sem=w_recv.at[q],
            device_id={"chan": dst}, device_id_type=MESH,
        )

    power[0] = jnp.zeros((rows, W), BF16)
    block(0)
    gap = iota((W, W), 0) - iota((W, W), 1)
    bands = [
        jnp.where(jnp.abs(gap + shift) <= HALF, 1.0, 0.0).astype(BF16) for shift in (-W, 0, W)
    ]

    def whiten(p, carry):
        block(p)
        q = p - 1
        window = dot(power[q], bands[0]) + dot(power[p], bands[1]) + dot(power[p + 1], bands[2])
        number = (jnp.minimum(q * W + iota((1, W), 1), HALF) + HALF + 1).astype(F32)
        factor = mask[...] * lax.rsqrt(window / number + EPS)
        own[q, :, :W] = (spec[q, :, :W] * factor).astype(BF16)
        own[q, :, W:] = (spec[q, :, W:] * factor).astype(BF16)

        @pl.when(has_dst)
        def _():
            white_copy(q).start()

        return carry

    lax.fori_loop(1, chunks + 1, whiten, 0)
    delay_copy.wait()
    total[...] = jnp.zeros_like(total)

    def correlate(q, carry):
        @pl.when(has_src)
        def _():
            white_copy(q).wait_recv()

        re = [None] * slots
        im = [None] * slots
        for s in range(segs):
            at = slice(s * W, (s + 1) * W)
            mine = own[q, at, :]
            pair = dot(sel[...], jnp.concatenate([mine, recv[q, at, :]], axis=0))
            my_re = mine[:, :W].astype(F32)
            my_im = mine[:, W:].astype(F32)
            for k in range(slots):
                pair_re = pair[k * W : (k + 1) * W, :W]
                pair_im = pair[k * W : (k + 1) * W, W:]
                one = my_re * pair_re + my_im * pair_im
                two = my_im * pair_re - my_re * pair_im
                re[k] = one if s == 0 else re[k] + one
                im[k] = two if s == 0 else im[k] + two
        for k in range(slots):
            cross = jnp.concatenate([re[k], im[k]], axis=1).astype(BF16)
            total[k] += dot(cross, dly[q])
        return carry

    lax.fori_loop(0, chunks, correlate, 0)

    gap = iota((W, W), 1) - iota((W, W), 0)
    sends_h = jnp.logical_and(up, z > 0)
    takes_h = jnp.logical_and(up, z < nz - 1)

    def h_copy(k):
        return pltpu.make_async_remote_copy(
            src_ref=hoth.at[k], dst_ref=hrecv.at[k], send_sem=h_send.at[k], recv_sem=h_recv.at[k],
            device_id={"chan": z - 1}, device_id_type=MESH,
        )

    def f_copy(k):
        return pltpu.make_async_remote_copy(
            src_ref=fsend.at[k], dst_ref=frecv.at[k], send_sem=f_send.at[k], recv_sem=f_recv.at[k],
            device_id={"freq": twin}, device_id_type=MESH,
        )

    def s_copy(k, d):
        peer = lax.rem(s_me + d, ns)
        return pltpu.make_async_remote_copy(
            src_ref=vsum.at[k, pl.ds(pl.multiple_of(peer * per, per), per)],
            dst_ref=srecv.at[d - 1, k], send_sem=s_send.at[d - 1, k], recv_sem=s_recv.at[d - 1, k],
            device_id={"seg": peer}, device_id_type=MESH,
        )

    @pl.when(up)
    def _():
        for k in range(slots):
            terms = total[k].astype(BF16)
            hoth[k] = dot(jnp.where(gap == offs[k] - W, 1.0, 0.0).astype(BF16), terms).astype(BF16)

            @pl.when(sends_h)
            def _():
                h_copy(k).start()

            total[k] = dot(jnp.where(gap == offs[k], 1.0, 0.0).astype(BF16), terms)

    half = LAGS // 2
    kept = pl.ds(pl.multiple_of(fq * half, half), half)
    given = pl.ds(pl.multiple_of(twin * half, half), half)
    for k in range(slots):
        @pl.when(takes_h)
        def _():
            h_copy(k).wait_recv()
            total[k] += hrecv[k].astype(F32)

        fsend[k] = total[k, :, given].astype(BF16)
        f_copy(k).start()
    for k in range(slots):
        f_copy(k).wait_recv()
        merged = total[k, :, kept] + frecv[k].astype(F32)
        total[k, :, kept] = merged
        vsum[k] = merged.astype(BF16)
        for d in range(1, ns):
            s_copy(k, d).start()
    for k in range(slots):
        result = total[k, pl.ds(pl.multiple_of(s_me * per, per), per), kept]
        for d in range(1, ns):
            s_copy(k, d).wait_recv()
            result += srecv[d - 1, k].astype(F32)
        out[k] = result

    @pl.when(has_dst)
    def _():
        def drain(q, carry):
            white_copy(q).wait_send()
            return carry

        lax.fori_loop(0, chunks, drain, 0)

    for k in range(slots):
        @pl.when(sends_h)
        def _():
            h_copy(k).wait_send()

        f_copy(k).wait_send()
        for d in range(1, ns):
            s_copy(k, d).wait_send()


def shards(traces, dead_mask, seg_counts, offsets):
    segs, chans, length = traces.shape
    nz, ns = lax.axis_size("chan"), lax.axis_size("seg")
    slots = offsets.shape[0]
    chunks = F // 2 // W
    rows = segs * chans
    per = chans // ns
    half = LAGS // 2
    vmem = pl.BlockSpec(memory_space=pltpu.VMEM)
    hbm = pl.BlockSpec(memory_space=pl.ANY)
    dma = pltpu.SemaphoreType.DMA
    terms = pl.pallas_call(
        functools.partial(kernel, nz, ns, segs, chunks, slots),
        out_shape=jax.ShapeDtypeStruct((slots, per, half), F32),
        in_specs=[pl.BlockSpec(memory_space=pltpu.SMEM), vmem, vmem, vmem, hbm, hbm],
        out_specs=vmem,
        scratch_shapes=[
            pltpu.VMEM((chunks + 1, length // 2, 2 * W), BF16),
            pltpu.VMEM((chunks, 2 * W, LAGS), BF16),
            pltpu.VMEM((chunks + 1, rows, 2 * W), F32),
            pltpu.VMEM((chunks + 2, rows, W), BF16),
            pltpu.VMEM((chunks, rows, 2 * W), BF16),
            pltpu.VMEM((chunks, rows, 2 * W), BF16),
            pltpu.VMEM((slots * W, 2 * W), BF16),
            pltpu.VMEM((rows, W), F32),
            pltpu.VMEM((slots, W, LAGS), F32),
            pltpu.VMEM((slots, W, LAGS), BF16),
            pltpu.VMEM((slots, W, LAGS), BF16),
            pltpu.VMEM((slots, W, half), BF16),
            pltpu.VMEM((slots, W, half), BF16),
            pltpu.VMEM((slots, W, half), BF16),
            pltpu.VMEM((max(ns - 1, 1), slots, per, half), BF16),
            dma((chunks + 1,)),
            dma,
            dma((chunks,)),
            dma((chunks,)),
            dma((slots,)),
            dma((slots,)),
            dma((slots,)),
            dma((slots,)),
            dma((max(ns - 1, 1), slots)),
            dma((max(ns - 1, 1), slots)),
        ],
        compiler_params=pltpu.CompilerParams(
            collective_id=0, has_side_effects=True, vmem_limit_bytes=56 * 1024 * 1024
        ),
    )(
        offsets,
        traces.reshape(rows, length),
        dead_mask.reshape(1, chans),
        seg_counts.reshape(1, chans),
        jnp.asarray(fourier_blocks(length, chunks)),
        jnp.asarray(delay_blocks(length, chunks)),
    )
    counts = seg_counts.astype(F32)
    after = lax.ppermute(counts, "chan", [(i + 1, i) for i in range(nz - 1)])
    both = jnp.concatenate([counts, after])
    first = lax.axis_index("seg") * per
    mine = lax.dynamic_slice_in_dim(counts, first, per)
    others = jnp.stack(
        [lax.dynamic_slice_in_dim(both, first + offsets[k], per) for k in range(slots)], axis=1
    )
    divisor = jnp.maximum(jnp.minimum(mine[:, None], others), 1.0)
    return jnp.transpose(terms, (1, 0, 2)) / divisor[:, :, None]


def solution(mesh):
    in_specs = (
        P("seg", ("groups", "chan"), None),
        P(("groups", "chan")),
        P(("groups", "chan")),
        P(),
    )
    out_specs = P(("groups", "chan", "seg"), None, "freq")
    return jax.shard_map(shards, mesh=mesh, in_specs=in_specs, out_specs=out_specs, check_vma=False)
```

time: 456 us -> 62.3 us (0.14)
  waiting for transfers between devices: 213 us -> 0.01 us
  other arithmetic: 165 us -> 1.73 us
  Pallas kernels: 0 us -> 54 us
  matrix products: 23.3 us -> 0 us
  local copies, waits for them, and re-layouts: 25.3 us -> 2.49 us
  between operations: 22.1 us -> 2.57 us
  starting transfers between devices: 6.67 us -> 1.28 us
    another operation x3 -> x0, other arithmetic: 117 us -> none
    ppermute x4 -> x1, waiting for transfers between devices: 108 us -> 0.01 us  [shards(): after = lax.ppermute(counts, 'chan', [(i + 1, i) for i in range(nz - 1)])]
    unnamed x3 -> x0, waiting for transfers between devices: 96.8 us -> none
    pallas_call x0 -> x1, Pallas kernels: none -> 54 us  [shards(): pl.pallas_call(functools.partial(kernel, nz, ns, segs, chunks, slots), ou...]
    dot_general x2 -> x0, matrix products: 23.3 us -> none  [the longest x1 17.7 us: shards(): jnp.dot(traces.reshape(seg_dev * chan_dev, length), fourier, preferred_el...]
    reduce_sum x1 -> x0, other arithmetic: 17.6 us -> none  [shards(): jnp.sum(white_re * partner_re + white_im * partner_im, axis=0)]
    mul x3 -> x0, other arithmetic: 13.8 us -> none  [the longest x1 9.73 us: delay_table(): jnp.cos(phases) * scaling]
    concatenate x4 -> x1, other arithmetic: 12.8 us -> 0.01 us  [shards(): both = jnp.concatenate([counts, after])]
  transfers between devices with their start and end apart: 6 -> 1, of which waited for: 4 -> 0; matrix products, arithmetic and copies ran while one was open for 2% -> 2% of each run, Pallas kernels for 0% -> 87%
where the time goes in v1:
time: 62.3 us; the launch traced here: 62.1 us
  Pallas kernels  54 us (87%)
  between operations  2.57 us (4%)
  local copies, waits for them, and re-layouts  2.49 us (4%)
  other arithmetic  1.73 us (3%)
  starting transfers between devices  1.28 us (2%)
    pallas_call x1, Pallas kernels, shards(): pl.pallas_call(functools.partial(kernel, nz, ns, segs, chunks, slots), ou...  54 us
    slice x1, local copies, waits for them, and re-layouts, shards(): offsets[k]  1.45 us
    ppermute x1, starting transfers between devices, shards(): after = lax.ppermute(counts, 'chan', [(i + 1, i) for i in range(nz - 1)])  1.28 us
  transfers between devices with their start and end apart: 1, of which 0 were waited for; matrix products, arithmetic and copies ran while one was open for 2% of the time, Pallas kernels for 87%

profile of v1, /device:TPU:0, one launch (start us, length us, event | category | flops | bytes accessed | tf_op | source)
XLA Modules:
  0.0 62.1 jit_solution(2523927957193405800)
XLA Ops:
  0.0 0.7 %convert_element_type.3 = f32[128]{0:T(128)S(1)} convert(s32[128]{0:T(128)} %param.8) | non-fusion elementwise | flops 128 | bytes 1024 | tf_op jit(solution)/shard_map/convert_element_type | solution.py:330
  0.7 1.3 %collective-permute-start = (f32[128]{0:T(128)S(1)}, f32[128]{0:T(128)S(1)}, u32[]{:S(2)}, u32[]{:S(2)}) collective-permute-start(f32[128]{0:T(128)S(1)} %convert_element_type.3), channel_id=1, source_target_pairs={{4,0},{8,4},{12,8},{5,1},{9,5},{13,9},{6,2},{10,6},{14,10},{7,3},{... | collective-permute-start | bytes 1544 | tf_op jit(solution)/shard_map/ppermute | solution.py:331
  1.9 1.5 %fusion.1 = (s32[1]{0:T(128)}, s32[1]{0:T(128)}, s32[1]{0:T(128)}, s32[1]{0:T(128)}) fusion(s32[4]{0:T(128)} %offs.1), kind=kLoop, calls=%fused_computation.8 | loop fusion | bytes 32 | tf_op jit(solution)/shard_map/slice | solution.py:336
  5.9 0.1 dynamic_slice.15
  6.0 54.0 %shard_map.64 = f32[4,64,256]{2,1,0:T(8,128)} custom-call(s32[4]{0:T(128)} %offs.1, bf16[640,4096]{1,0:T(8,128)(2,1)} %bitcast.17, s32[1,128]{1,0:T(1,128)} %bitcast.18, s32[1,128]{1,0:T(1,128)} %bitcast.19, bf16[2,9,2048,256]{3,2,1,0:T(8,128)(2,1)} %constant.18.clone.four, bf16[2,8,256,512]{3,2,1,0:T(8,128)(2,1)} %constant.19.clone.delay), custom_call_target="tpu_custom_call" | custom-call | tf_op jit(solution)/shard_map/pallas_call | solution.py:287
  60.1 0.0 collective-permute-done
  60.1 0.1 dynamic-slice_bitcast_fusion.3
  60.2 1.1 %bitcast_divide_fusion = f32[64,4,256]{2,0,1:T(8,128)S(1)} fusion(f32[4,64,256]{2,1,0:T(8,128)} %shard_map.64, f32[64,4]{0,1:T(4,128)S(1)} %fusion), kind=kLoop, calls=%fused_computation | loop fusion | flops 65536 | bytes 525312 | tf_op jit(solution)/shard_map/div | solution.py:339
  61.2 0.9 %copy.7 = f32[64,4,256]{2,1,0:T(4,128)} copy(f32[64,4,256]{2,0,1:T(8,128)S(1)} %bitcast_divide_fusion) | data formatting | bytes 524288 | tf_op jit(solution)/shard_map/div | solution.py:339
  (2 shorter events, 0.0 us)
Async XLA Ops:
  0.7 59.4 %collective-permute-start = (f32[128]{0:T(128)S(1)}, f32[128]{0:T(128)S(1)}, u32[]{:S(2)}, u32[]{:S(2)}) collective-permute-start(f32[128]{0:T(128)S(1)} %convert_element_type.3), channel_id=1, source_target_pairs={{4,0},{8,4},{12,8},{5,1},{9,5},{13,9},{6,2},{10,6},{14,10},{7,3},{... | collective-permute-start | bytes 1544 | tf_op jit(solution)/shard_map/ppermute | solution.py:331

commit v2 on v1

--- a/solution.py
+++ b/solution.py
@@ -59,9 +59,9 @@
 
 
 def kernel(
-    nz, ns, segs, chunks, slots, offs, tr, dead, cnt, four, delay, out,
-    table, dly, spec, power, own, recv, sel, mask, total, hoth, hrecv, fsend, frecv, vsum, srecv,
-    tab_sem, dly_sem, w_send, w_recv, h_send, h_recv, f_send, f_recv, s_send, s_recv,
+    nz, ns, segs, chunks, slots, offs, traces, dead, cnt, four, delay, out,
+    tr, crecv, inverse, table, dly, spec, power, own, recv, sel, mask, total, hoth, hrecv, fsend, frecv, vsum, srecv,
+    tr_sem, c_send, c_recv, tab_sem, dly_sem, w_send, w_recv, h_send, h_recv, f_send, f_recv, s_send, s_recv,
 ):
     z = lax.axis_index("chan")
     s_me = lax.axis_index("seg")
@@ -80,7 +80,15 @@
     def table_copy(p):
         return pltpu.make_async_copy(four.at[fq, p], table.at[p], tab_sem.at[p])
 
-    for p in range(chunks + 1):
+    def trace_copy(s):
+        return pltpu.make_async_copy(
+            traces.at[pl.ds(s * W, W)], tr.at[pl.ds(s * W, W)], tr_sem.at[s]
+        )
+
+    table_copy(0).start()
+    for s in range(segs):
+        trace_copy(s).start()
+    for p in range(1, chunks + 1):
         table_copy(p).start()
     delay_copy = pltpu.make_async_copy(delay.at[fq], dly, dly_sem)
     delay_copy.start()
@@ -100,9 +108,6 @@
         pl.semaphore_signal(
             barrier, inc=1, device_id={"seg": lax.rem(s_me + d, ns)}, device_id_type=MESH
         )
-
-    peers = ns + has_dst.astype(jnp.int32) + has_src.astype(jnp.int32)
-    pl.semaphore_wait(barrier, peers)
 
     diag = iota((W, W), 0) == iota((W, W), 1)
     cnt_col = jnp.sum(jnp.where(diag, cnt[...], 0).astype(F32), axis=1, keepdims=True)
@@ -122,6 +127,7 @@
             return carry
 
         lax.fori_loop(0, chunks, clear, 0)
+        crecv[...] = jnp.zeros_like(crecv)
 
     parity = (iota((1, 2 * W), 1) & 1).astype(F32)
     parity = (1.0 - 2.0 * parity) * (1 - 2 * fq).astype(F32)
@@ -141,8 +147,21 @@
             device_id={"chan": dst}, device_id_type=MESH,
         )
 
+    count_copy = pltpu.make_async_remote_copy(
+        src_ref=cnt, dst_ref=crecv, send_sem=c_send, recv_sem=c_recv,
+        device_id={"chan": dst}, device_id_type=MESH,
+    )
     power[0] = jnp.zeros((rows, W), BF16)
+    for s in range(segs):
+        trace_copy(s).wait()
     block(0)
+    peers = ns + has_dst.astype(jnp.int32) + has_src.astype(jnp.int32)
+    pl.semaphore_wait(barrier, peers)
+
+    @pl.when(has_dst)
+    def _():
+        count_copy.start()
+
     gap = iota((W, W), 0) - iota((W, W), 1)
     bands = [
         jnp.where(jnp.abs(gap + shift) <= HALF, 1.0, 0.0).astype(BF16) for shift in (-W, 0, W)
@@ -166,6 +185,17 @@
     lax.fori_loop(1, chunks + 1, whiten, 0)
     delay_copy.wait()
     total[...] = jnp.zeros_like(total)
+
+    @pl.when(has_src)
+    def _():
+        count_copy.wait_recv()
+
+    counts = jnp.concatenate([cnt[...], crecv[...]], axis=1)
+    for k in range(slots):
+        target = (iota((W, 2 * W), 0) - step * offs[k] + 2 * W) & (2 * W - 1)
+        partner = jnp.where(iota((W, 2 * W), 1) == target, counts, 0).astype(F32)
+        fewer = jnp.minimum(cnt_col, jnp.sum(partner, axis=1, keepdims=True))
+        inverse[k] = jnp.broadcast_to(1.0 / jnp.maximum(fewer, 1.0), (W, W))
 
     def correlate(q, carry):
         @pl.when(has_src)
@@ -188,7 +218,8 @@
                 re[k] = one if s == 0 else re[k] + one
                 im[k] = two if s == 0 else im[k] + two
         for k in range(slots):
-            cross = jnp.concatenate([re[k], im[k]], axis=1).astype(BF16)
+            scale = inverse[k]
+            cross = jnp.concatenate([re[k] * scale, im[k] * scale], axis=1).astype(BF16)
             total[k] += dot(cross, dly[q])
         return carry
 
@@ -253,7 +284,7 @@
         for d in range(1, ns):
             s_copy(k, d).wait_recv()
             result += srecv[d - 1, k].astype(F32)
-        out[k] = result
+        out[:, k, :] = result
 
     @pl.when(has_dst)
     def _():
@@ -262,6 +293,7 @@
             return carry
 
         lax.fori_loop(0, chunks, drain, 0)
+        count_copy.wait_send()
 
     for k in range(slots):
         @pl.when(sends_h)
@@ -284,12 +316,15 @@
     vmem = pl.BlockSpec(memory_space=pltpu.VMEM)
     hbm = pl.BlockSpec(memory_space=pl.ANY)
     dma = pltpu.SemaphoreType.DMA
-    terms = pl.pallas_call(
+    return pl.pallas_call(
         functools.partial(kernel, nz, ns, segs, chunks, slots),
-        out_shape=jax.ShapeDtypeStruct((slots, per, half), F32),
-        in_specs=[pl.BlockSpec(memory_space=pltpu.SMEM), vmem, vmem, vmem, hbm, hbm],
+        out_shape=jax.ShapeDtypeStruct((per, slots, half), F32),
+        in_specs=[pl.BlockSpec(memory_space=pltpu.SMEM), hbm, vmem, vmem, hbm, hbm],
         out_specs=vmem,
         scratch_shapes=[
+            pltpu.VMEM((rows, length), BF16),
+            pltpu.VMEM((1, chans), jnp.int32),
+            pltpu.VMEM((slots, W, W), F32),
             pltpu.VMEM((chunks + 1, length // 2, 2 * W), BF16),
             pltpu.VMEM((chunks, 2 * W, LAGS), BF16),
             pltpu.VMEM((chunks + 1, rows, 2 * W), F32),
@@ -305,6 +340,9 @@
             pltpu.VMEM((slots, W, half), BF16),
             pltpu.VMEM((slots, W, half), BF16),
             pltpu.VMEM((max(ns - 1, 1), slots, per, half), BF16),
+            dma((segs,)),
+            dma,
+            dma,
             dma((chunks + 1,)),
             dma,
             dma((chunks,)),
@@ -327,16 +365,6 @@
         jnp.asarray(fourier_blocks(length, chunks)),
         jnp.asarray(delay_blocks(length, chunks)),
     )
-    counts = seg_counts.astype(F32)
-    after = lax.ppermute(counts, "chan", [(i + 1, i) for i in range(nz - 1)])
-    both = jnp.concatenate([counts, after])
-    first = lax.axis_index("seg") * per
-    mine = lax.dynamic_slice_in_dim(counts, first, per)
-    others = jnp.stack(
-        [lax.dynamic_slice_in_dim(both, first + offsets[k], per) for k in range(slots)], axis=1
-    )
-    divisor = jnp.maximum(jnp.minimum(mine[:, None], others), 1.0)
-    return jnp.transpose(terms, (1, 0, 2)) / divisor[:, :, None]
 
 
 def solution(mesh):

time: 62.3 us -> 56.3 us (0.904)
  between operations: 2.57 us -> 0.01 us
  other arithmetic: 1.73 us -> 0 us
  starting transfers between devices: 1.28 us -> 0 us
  local copies, waits for them, and re-layouts: 2.49 us -> 1.67 us
    unnamed x0 -> x1, local copies, waits for them, and re-layouts: none -> 1.67 us
    slice x1 -> x0, local copies, waits for them, and re-layouts: 1.45 us -> none  [shards(): offsets[k]]
    ppermute x1 -> x0, starting transfers between devices: 1.28 us -> none  [shards(): after = lax.ppermute(counts, 'chan', [(i + 1, i) for i in range(nz - 1)])]
    div x1 -> x0, other arithmetic: 1.05 us -> none  [shards(): return jnp.transpose(terms, (1, 0, 2)) / divisor[:, :, None]]
    div x1 -> x0, local copies, waits for them, and re-layouts: 0.87 us -> none  [shards(): return jnp.transpose(terms, (1, 0, 2)) / divisor[:, :, None]]
    convert_element_type x1 -> x0, other arithmetic: 0.66 us -> none  [shards(): counts = seg_counts.astype(F32)]
  transfers between devices with their start and end apart: 1 -> 0, of which waited for: 0 -> 0; matrix products, arithmetic and copies ran while one was open for 2% -> 0% of each run, Pallas kernels for 87% -> 0%
where the time goes in v2:
time: 56.3 us; the launch traced here: 56.1 us
  Pallas kernels  54.4 us (97%)
  local copies, waits for them, and re-layouts  1.67 us (3%)
    pallas_call x1, Pallas kernels, shards(): pl.pallas_call(functools.partial(kernel, nz, ns, segs, chunks, slots), ou...  54.4 us
    unnamed x1, local copies, waits for them, and re-layouts  1.67 us

profile of v2, /device:TPU:0, one launch (start us, length us, event | category | flops | bytes accessed | tf_op | source)
XLA Modules:
  0.0 56.1 jit_solution(2061997818769180336)
XLA Ops:
  0.0 54.4 %shard_map.64 = f32[64,4,256]{2,1,0:T(4,128)} custom-call(s32[4]{0:T(128)} %offs.1, bf16[640,4096]{1,0:T(8,128)(2,1)} %bitcast.3, s32[1,128]{1,0:T(1,128)} %bitcast.4, s32[1,128]{1,0:T(1,128)} %bitcast.5, bf16[2,9,2048,256]{3,2,1,0:T(8,128)(2,1)} %constant.4.clone.four, bf16[2,8,256,512]{3,2,1,0:T(8,128)(2,1)} %constant.5.clone.delay), custom_call_target="tpu_custom_call" | custom-call | tf_op jit(solution)/shard_map/pallas_call | solution.py:319
  54.4 1.7 %copy.8 = f32[64,4,256]{2,1,0:T(4,128)} copy(f32[64,4,256]{2,1,0:T(4,128)} %shard_map.64) | data formatting | bytes 524288

commit v3 on v2

--- a/solution.py
+++ b/solution.py
@@ -93,11 +93,9 @@
     delay_copy = pltpu.make_async_copy(delay.at[fq], dly, dly_sem)
     delay_copy.start()
 
+    sends_h = jnp.logical_and(up, z > 0)
+    takes_h = z < nz - 1
     barrier = pltpu.get_barrier_semaphore()
-
-    @pl.when(has_dst)
-    def _():
-        pl.semaphore_signal(barrier, inc=1, device_id={"chan": dst}, device_id_type=MESH)
 
     @pl.when(has_src)
     def _():
@@ -108,6 +106,12 @@
         pl.semaphore_signal(
             barrier, inc=1, device_id={"seg": lax.rem(s_me + d, ns)}, device_id_type=MESH
         )
+
+    @pl.when(takes_h)
+    def _():
+        for d in range(ns):
+            giver = {"chan": z + 1, "seg": lax.rem(s_me + d, ns), "freq": 1}
+            pl.semaphore_signal(barrier, inc=1, device_id=giver, device_id_type=MESH)
 
     diag = iota((W, W), 0) == iota((W, W), 1)
     cnt_col = jnp.sum(jnp.where(diag, cnt[...], 0).astype(F32), axis=1, keepdims=True)
@@ -128,6 +132,10 @@
 
         lax.fori_loop(0, chunks, clear, 0)
         crecv[...] = jnp.zeros_like(crecv)
+
+    @pl.when(jnp.logical_not(takes_h))
+    def _():
+        hrecv[...] = jnp.zeros_like(hrecv)
 
     parity = (iota((1, 2 * W), 1) & 1).astype(F32)
     parity = (1.0 - 2.0 * parity) * (1 - 2 * fq).astype(F32)
@@ -155,7 +163,7 @@
     for s in range(segs):
         trace_copy(s).wait()
     block(0)
-    peers = ns + has_dst.astype(jnp.int32) + has_src.astype(jnp.int32)
+    peers = ns + has_dst.astype(jnp.int32) + 2 * ns * sends_h.astype(jnp.int32)
     pl.semaphore_wait(barrier, peers)
 
     @pl.when(has_dst)
@@ -226,65 +234,71 @@
     lax.fori_loop(0, chunks, correlate, 0)
 
     gap = iota((W, W), 1) - iota((W, W), 0)
-    sends_h = jnp.logical_and(up, z > 0)
-    takes_h = jnp.logical_and(up, z < nz - 1)
-
-    def h_copy(k):
-        return pltpu.make_async_remote_copy(
-            src_ref=hoth.at[k], dst_ref=hrecv.at[k], send_sem=h_send.at[k], recv_sem=h_recv.at[k],
-            device_id={"chan": z - 1}, device_id_type=MESH,
-        )
-
-    def f_copy(k):
-        return pltpu.make_async_remote_copy(
-            src_ref=fsend.at[k], dst_ref=frecv.at[k], send_sem=f_send.at[k], recv_sem=f_recv.at[k],
-            device_id={"freq": twin}, device_id_type=MESH,
-        )
-
-    def s_copy(k, d):
+    half = LAGS // 2
+
+    def h_copy(d, q):
         peer = lax.rem(s_me + d, ns)
         return pltpu.make_async_remote_copy(
-            src_ref=vsum.at[k, pl.ds(pl.multiple_of(peer * per, per), per)],
-            dst_ref=srecv.at[d - 1, k], send_sem=s_send.at[d - 1, k], recv_sem=s_recv.at[d - 1, k],
+            src_ref=hoth.at[:, pl.ds(pl.multiple_of(peer * per, per), per), q * half : (q + 1) * half],
+            dst_ref=hrecv.at[d], send_sem=h_send.at[d, q], recv_sem=h_recv.at[d],
+            device_id={"chan": z - 1, "seg": peer, "freq": q}, device_id_type=MESH,
+        )
+
+    f_copy = pltpu.make_async_remote_copy(
+        src_ref=fsend, dst_ref=frecv, send_sem=f_send, recv_sem=f_recv,
+        device_id={"freq": twin}, device_id_type=MESH,
+    )
+
+    def s_copy(d):
+        peer = lax.rem(s_me + d, ns)
+        return pltpu.make_async_remote_copy(
+            src_ref=vsum.at[:, pl.ds(pl.multiple_of(peer * per, per), per)],
+            dst_ref=srecv.at[d - 1], send_sem=s_send.at[d - 1], recv_sem=s_recv.at[d - 1],
             device_id={"seg": peer}, device_id_type=MESH,
         )
 
     @pl.when(up)
     def _():
         for k in range(slots):
-            terms = total[k].astype(BF16)
-            hoth[k] = dot(jnp.where(gap == offs[k] - W, 1.0, 0.0).astype(BF16), terms).astype(BF16)
-
-            @pl.when(sends_h)
-            def _():
-                h_copy(k).start()
-
-            total[k] = dot(jnp.where(gap == offs[k], 1.0, 0.0).astype(BF16), terms)
-
-    half = LAGS // 2
+            moved = dot(jnp.where(gap == offs[k] - W, 1.0, 0.0).astype(BF16), total[k].astype(BF16))
+            hoth[k] = moved.astype(BF16)
+
+        @pl.when(sends_h)
+        def _():
+            for d in reversed(range(ns)):
+                for q in range(2):
+                    h_copy(d, q).start()
+
+        for k in range(slots):
+            total[k] = dot(jnp.where(gap == offs[k], 1.0, 0.0).astype(BF16), total[k].astype(BF16))
+
     kept = pl.ds(pl.multiple_of(fq * half, half), half)
     given = pl.ds(pl.multiple_of(twin * half, half), half)
     for k in range(slots):
-        @pl.when(takes_h)
-        def _():
-            h_copy(k).wait_recv()
-            total[k] += hrecv[k].astype(F32)
-
         fsend[k] = total[k, :, given].astype(BF16)
-        f_copy(k).start()
-    for k in range(slots):
-        f_copy(k).wait_recv()
+    f_copy.start()
+    f_copy.wait_recv()
+    for k in range(slots):
         merged = total[k, :, kept] + frecv[k].astype(F32)
         total[k, :, kept] = merged
         vsum[k] = merged.astype(BF16)
-        for d in range(1, ns):
-            s_copy(k, d).start()
+    for d in range(1, ns):
+        s_copy(d).start()
+    for d in range(1, ns):
+        s_copy(d).wait_recv()
+
+    @pl.when(takes_h)
+    def _():
+        for d in range(ns):
+            h_copy(d, 0).wait_recv()
+
     for k in range(slots):
         result = total[k, pl.ds(pl.multiple_of(s_me * per, per), per), kept]
         for d in range(1, ns):
-            s_copy(k, d).wait_recv()
             result += srecv[d - 1, k].astype(F32)
-        out[:, k, :] = result
+        for d in range(ns):
+            result += hrecv[d, k].astype(F32)
+        out[k] = result
 
     @pl.when(has_dst)
     def _():
@@ -295,14 +309,15 @@
         lax.fori_loop(0, chunks, drain, 0)
         count_copy.wait_send()
 
-    for k in range(slots):
-        @pl.when(sends_h)
-        def _():
-            h_copy(k).wait_send()
-
-        f_copy(k).wait_send()
-        for d in range(1, ns):
-            s_copy(k, d).wait_send()
+    @pl.when(sends_h)
+    def _():
+        for d in range(ns):
+            for q in range(2):
+                h_copy(d, q).wait_send()
+
+    f_copy.wait_send()
+    for d in range(1, ns):
+        s_copy(d).wait_send()
 
 
 def shards(traces, dead_mask, seg_counts, offsets):
@@ -316,9 +331,9 @@
     vmem = pl.BlockSpec(memory_space=pltpu.VMEM)
     hbm = pl.BlockSpec(memory_space=pl.ANY)
     dma = pltpu.SemaphoreType.DMA
-    return pl.pallas_call(
+    terms = pl.pallas_call(
         functools.partial(kernel, nz, ns, segs, chunks, slots),
-        out_shape=jax.ShapeDtypeStruct((per, slots, half), F32),
+        out_shape=jax.ShapeDtypeStruct((slots, per, half), F32),
         in_specs=[pl.BlockSpec(memory_space=pltpu.SMEM), hbm, vmem, vmem, hbm, hbm],
         out_specs=vmem,
         scratch_shapes=[
@@ -335,7 +350,7 @@
             pltpu.VMEM((rows, W), F32),
             pltpu.VMEM((slots, W, LAGS), F32),
             pltpu.VMEM((slots, W, LAGS), BF16),
-            pltpu.VMEM((slots, W, LAGS), BF16),
+            pltpu.VMEM((ns, slots, per, half), BF16),
             pltpu.VMEM((slots, W, half), BF16),
             pltpu.VMEM((slots, W, half), BF16),
             pltpu.VMEM((slots, W, half), BF16),
@@ -347,12 +362,12 @@
             dma,
             dma((chunks,)),
             dma((chunks,)),
-            dma((slots,)),
-            dma((slots,)),
-            dma((slots,)),
-            dma((slots,)),
-            dma((max(ns - 1, 1), slots)),
-            dma((max(ns - 1, 1), slots)),
+            dma((ns, 2)),
+            dma((ns,)),
+            dma,
+            dma,
+            dma((max(ns - 1, 1),)),
+            dma((max(ns - 1, 1),)),
         ],
         compiler_params=pltpu.CompilerParams(
             collective_id=0, has_side_effects=True, vmem_limit_bytes=56 * 1024 * 1024
@@ -365,6 +380,7 @@
         jnp.asarray(fourier_blocks(length, chunks)),
         jnp.asarray(delay_blocks(length, chunks)),
     )
+    return jnp.transpose(terms, (1, 0, 2))
 
 
 def solution(mesh):

time: 56.3 us -> 53 us (0.941)
  Pallas kernels: 54.4 us -> 51 us
    pallas_call x1, Pallas kernels: 54.4 us -> 51 us  [shards(): pl.pallas_call(functools.partial(kernel, nz, ns, segs, chunks, slots), ou...]
    transpose x0 -> x1, local copies, waits for them, and re-layouts: none -> 1.82 us  [shards(): return jnp.transpose(terms, (1, 0, 2))]
    unnamed x1 -> x0, local copies, waits for them, and re-layouts: 1.67 us -> none
where the time goes in v3:
time: 53 us; the launch traced here: 52.8 us
  Pallas kernels  51 us (96%)
  local copies, waits for them, and re-layouts  1.82 us (3%)
    pallas_call x1, Pallas kernels, shards(): pl.pallas_call(functools.partial(kernel, nz, ns, segs, chunks, slots), ou...  51 us
    transpose x1, local copies, waits for them, and re-layouts, shards(): return jnp.transpose(terms, (1, 0, 2))  1.82 us

profile of v3, /device:TPU:0, one launch (start us, length us, event | category | flops | bytes accessed | tf_op | source)
XLA Modules:
  0.0 52.8 jit_solution(14590029019734066407)
XLA Ops:
  0.0 51.0 %shard_map.64 = f32[4,64,256]{2,1,0:T(8,128)} custom-call(s32[4]{0:T(128)} %offs.1, bf16[640,4096]{1,0:T(8,128)(2,1)} %bitcast.4, s32[1,128]{1,0:T(1,128)} %bitcast.6, s32[1,128]{1,0:T(1,128)} %bitcast.7, bf16[2,9,2048,256]{3,2,1,0:T(8,128)(2,1)} %constant.4.clone.four, bf16[2,8,256,512]{3,2,1,0:T(8,128)(2,1)} %constant.5.clone.delay), custom_call_target="tpu_custom_call" | custom-call | tf_op jit(solution)/shard_map/pallas_call | solution.py:334
  51.0 1.8 %copy.7 = f32[64,4,256]{2,1,0:T(4,128)} copy(f32[64,4,256]{2,0,1:T(8,128)} %bitcast.5) | data formatting | bytes 524288 | tf_op jit(solution)/shard_map/transpose | solution.py:383

commit v4 on v3

--- a/solution.py
+++ b/solution.py
@@ -86,9 +86,11 @@
         )
 
     table_copy(0).start()
-    for s in range(segs):
+    trace_copy(0).start()
+    table_copy(1).start()
+    for s in range(1, segs):
         trace_copy(s).start()
-    for p in range(1, chunks + 1):
+    for p in range(2, chunks + 1):
         table_copy(p).start()
     delay_copy = pltpu.make_async_copy(delay.at[fq], dly, dly_sem)
     delay_copy.start()
@@ -140,29 +142,57 @@
     parity = (iota((1, 2 * W), 1) & 1).astype(F32)
     parity = (1.0 - 2.0 * parity) * (1 - 2 * fq).astype(F32)
 
-    def block(p):
-        table_copy(p).wait()
-        first = dot(tr[:, :half_len], table[p])
-        second = dot(tr[:, half_len:], table[p])
+    gap = iota((W, W), 0) - iota((W, W), 1)
+    bands = [
+        jnp.where(jnp.abs(gap + shift) <= HALF, 1.0, 0.0).astype(BF16) for shift in (-W, 0, W)
+    ]
+
+    def block(p, at):
+        first = dot(tr[at, :half_len], table[p])
+        second = dot(tr[at, half_len:], table[p])
         both = first + parity * second
-        spec[p] = both
+        spec[p, at, :] = both
         square = both * both
-        power[p + 1] = (square[:, :W] + square[:, W:]).astype(BF16)
-
-    def white_copy(q):
+        power[p + 1, at, :] = (square[:, :W] + square[:, W:]).astype(BF16)
+
+    def whiten(q, at):
+        window = (
+            dot(power[q, at, :], bands[0]) + dot(power[q + 1, at, :], bands[1])
+            + dot(power[q + 2, at, :], bands[2])
+        )
+        number = (jnp.minimum(q * W + iota((1, W), 1), HALF) + HALF + 1).astype(F32)
+        factor = mask[at, :] * lax.rsqrt(window / number + EPS)
+        own[q, at, :W] = (spec[q, at, :W] * factor).astype(BF16)
+        own[q, at, W:] = (spec[q, at, W:] * factor).astype(BF16)
+
+    def white_copy(q, at):
         return pltpu.make_async_remote_copy(
-            src_ref=own.at[q], dst_ref=recv.at[q], send_sem=w_send.at[q], recv_sem=w_recv.at[q],
+            src_ref=own.at[q, at], dst_ref=recv.at[q, at],
+            send_sem=w_send.at[q], recv_sem=w_recv.at[q],
             device_id={"chan": dst}, device_id_type=MESH,
         )
+
+    def send(q, at):
+        @pl.when(has_dst)
+        def _():
+            white_copy(q, at).start()
+
+    whole = pl.ds(0, rows)
+
+    def rows_of(s):
+        return pl.ds(pl.multiple_of(s * W, W), W)
 
     count_copy = pltpu.make_async_remote_copy(
         src_ref=cnt, dst_ref=crecv, send_sem=c_send, recv_sem=c_recv,
         device_id={"chan": dst}, device_id_type=MESH,
     )
     power[0] = jnp.zeros((rows, W), BF16)
-    for s in range(segs):
-        trace_copy(s).wait()
-    block(0)
+    table_copy(0).wait()
+    trace_copy(0).wait()
+    block(0, rows_of(0))
+    table_copy(1).wait()
+    block(1, rows_of(0))
+    whiten(0, rows_of(0))
     peers = ns + has_dst.astype(jnp.int32) + 2 * ns * sends_h.astype(jnp.int32)
     pl.semaphore_wait(barrier, peers)
 
@@ -170,27 +200,33 @@
     def _():
         count_copy.start()
 
-    gap = iota((W, W), 0) - iota((W, W), 1)
-    bands = [
-        jnp.where(jnp.abs(gap + shift) <= HALF, 1.0, 0.0).astype(BF16) for shift in (-W, 0, W)
-    ]
-
-    def whiten(p, carry):
-        block(p)
-        q = p - 1
-        window = dot(power[q], bands[0]) + dot(power[p], bands[1]) + dot(power[p + 1], bands[2])
-        number = (jnp.minimum(q * W + iota((1, W), 1), HALF) + HALF + 1).astype(F32)
-        factor = mask[...] * lax.rsqrt(window / number + EPS)
-        own[q, :, :W] = (spec[q, :, :W] * factor).astype(BF16)
-        own[q, :, W:] = (spec[q, :, W:] * factor).astype(BF16)
-
-        @pl.when(has_dst)
-        def _():
-            white_copy(q).start()
-
+    send(0, rows_of(0))
+
+    def first_chunk(s, carry):
+        trace_copy(s).wait()
+        block(0, rows_of(s))
+        block(1, rows_of(s))
+        whiten(0, rows_of(s))
+        send(0, rows_of(s))
         return carry
 
-    lax.fori_loop(1, chunks + 1, whiten, 0)
+    def second_chunk(s, carry):
+        block(2, rows_of(s))
+        whiten(1, rows_of(s))
+        send(1, rows_of(s))
+        return carry
+
+    def later_chunk(p, carry):
+        table_copy(p).wait()
+        block(p, whole)
+        whiten(p - 1, whole)
+        send(p - 1, whole)
+        return carry
+
+    lax.fori_loop(1, segs, first_chunk, 0)
+    table_copy(2).wait()
+    lax.fori_loop(0, segs, second_chunk, 0)
+    lax.fori_loop(3, chunks + 1, later_chunk, 0)
     delay_copy.wait()
     total[...] = jnp.zeros_like(total)
 
@@ -208,7 +244,7 @@
     def correlate(q, carry):
         @pl.when(has_src)
         def _():
-            white_copy(q).wait_recv()
+            white_copy(q, whole).wait_recv()
 
         re = [None] * slots
         im = [None] * slots
@@ -303,7 +339,7 @@
     @pl.when(has_dst)
     def _():
         def drain(q, carry):
-            white_copy(q).wait_send()
+            white_copy(q, whole).wait_send()
             return carry
 
         lax.fori_loop(0, chunks, drain, 0)

time: 53 us -> 49.8 us (0.940)
  Pallas kernels: 51 us -> 47.9 us
    pallas_call x1, Pallas kernels: 51 us -> 47.9 us  [shards(): pl.pallas_call(functools.partial(kernel, nz, ns, segs, chunks, slots), ou...]
where the time goes in v4:
time: 49.8 us; the launch traced here: 49.7 us
  Pallas kernels  47.9 us (96%)
  local copies, waits for them, and re-layouts  1.82 us (4%)
    pallas_call x1, Pallas kernels, shards(): pl.pallas_call(functools.partial(kernel, nz, ns, segs, chunks, slots), ou...  47.9 us
    transpose x1, local copies, waits for them, and re-layouts, shards(): return jnp.transpose(terms, (1, 0, 2))  1.82 us

profile of v4, /device:TPU:0, one launch (start us, length us, event | category | flops | bytes accessed | tf_op | source)
XLA Modules:
  0.0 49.7 jit_solution(6094674864772767570)
XLA Ops:
  0.0 47.9 %shard_map.64 = f32[4,64,256]{2,1,0:T(8,128)} custom-call(s32[4]{0:T(128)} %offs.1, bf16[640,4096]{1,0:T(8,128)(2,1)} %bitcast.4, s32[1,128]{1,0:T(1,128)} %bitcast.6, s32[1,128]{1,0:T(1,128)} %bitcast.7, bf16[2,9,2048,256]{3,2,1,0:T(8,128)(2,1)} %constant.4.clone.four, bf16[2,8,256,512]{3,2,1,0:T(8,128)(2,1)} %constant.5.clone.delay), custom_call_target="tpu_custom_call" | custom-call | tf_op jit(solution)/shard_map/pallas_call | solution.py:370
  47.9 1.8 %copy.7 = f32[64,4,256]{2,1,0:T(4,128)} copy(f32[64,4,256]{2,0,1:T(8,128)} %bitcast.5) | data formatting | bytes 524288 | tf_op jit(solution)/shard_map/transpose | solution.py:419

commit v5 on v4

--- a/solution.py
+++ b/solution.py
@@ -210,10 +210,10 @@
         send(0, rows_of(s))
         return carry
 
-    def second_chunk(s, carry):
-        block(2, rows_of(s))
-        whiten(1, rows_of(s))
-        send(1, rows_of(s))
+    def early_chunk(p, s, carry):
+        block(p, rows_of(s))
+        whiten(p - 1, rows_of(s))
+        send(p - 1, rows_of(s))
         return carry
 
     def later_chunk(p, carry):
@@ -224,9 +224,10 @@
         return carry
 
     lax.fori_loop(1, segs, first_chunk, 0)
-    table_copy(2).wait()
-    lax.fori_loop(0, segs, second_chunk, 0)
-    lax.fori_loop(3, chunks + 1, later_chunk, 0)
+    for p in range(2, 4):
+        table_copy(p).wait()
+        lax.fori_loop(0, segs, functools.partial(early_chunk, p), 0)
+    lax.fori_loop(4, chunks + 1, later_chunk, 0)
     delay_copy.wait()
     total[...] = jnp.zeros_like(total)
 

time: 49.8 us -> 49.5 us (level)
  no operation moved by 1% of the time
where the time goes in v5:
time: 49.5 us; the launch traced here: 49.3 us
  Pallas kernels  47.5 us (96%)
  local copies, waits for them, and re-layouts  1.82 us (4%)
    pallas_call x1, Pallas kernels, shards(): pl.pallas_call(functools.partial(kernel, nz, ns, segs, chunks, slots), ou...  47.5 us
    transpose x1, local copies, waits for them, and re-layouts, shards(): return jnp.transpose(terms, (1, 0, 2))  1.82 us

profile of v5, /device:TPU:0, one launch (start us, length us, event | category | flops | bytes accessed | tf_op | source)
XLA Modules:
  0.0 49.3 jit_solution(1293516480227297298)
XLA Ops:
  0.0 47.5 %shard_map.64 = f32[4,64,256]{2,1,0:T(8,128)} custom-call(s32[4]{0:T(128)} %offs.1, bf16[640,4096]{1,0:T(8,128)(2,1)} %bitcast.4, s32[1,128]{1,0:T(1,128)} %bitcast.6, s32[1,128]{1,0:T(1,128)} %bitcast.7, bf16[2,9,2048,256]{3,2,1,0:T(8,128)(2,1)} %constant.4.clone.four, bf16[2,8,256,512]{3,2,1,0:T(8,128)(2,1)} %constant.5.clone.delay), custom_call_target="tpu_custom_call" | custom-call | tf_op jit(solution)/shard_map/pallas_call | solution.py:371
  47.5 1.8 %copy.7 = f32[64,4,256]{2,1,0:T(4,128)} copy(f32[64,4,256]{2,0,1:T(8,128)} %bitcast.5) | data formatting | bytes 524288 | tf_op jit(solution)/shard_map/transpose | solution.py:420
